TPU v7x, 256 devices: a whole 4x4x8 slice. The times are simulated.
256 devices in a mesh: sub: 4 (over z_hi), row: 16 (over y, x), col: 4 (over z_lo, core).
Axes of the slice: x: 4, y: 4, z: 8 (z_hi: 4, z_lo: 2; z = z_hi * 2 + z_lo), core: 2. Of those that a mesh axis runs over, the one named last changes fastest.
Arguments:
- front_in: float32 [12288, 12288], P('row', ('sub', 'col')), as said below
- child_updates: float32 [4, 8192, 8192], P('sub', 'row', 'col'), as said below
- pattern: int32 [4, 32, 32], P('sub', 'row', 'col'), may hold values from 0 to 1, as said below
- child_map: int32 [4, 32], replicated, may hold values from 0 to 47, as said below
- pivot_inverse: float32 [1024, 1024], replicated, as said below
Outputs:
- front_out: float32 [12288, 12288], P('row', ('sub', 'col'))
Inputs may be any that keep to these rules, and one draw needn't show every extreme that they name: front_in is symmetric. Each child_updates[s] is symmetric. Each pattern[s] is symmetric. child_map[s] is strictly increasing, and child_map[s, i] // 3 equals i // 2. pivot_inverse is lower triangular with a positive diagonal.
All inputs are finite; a program needn't handle non-finite values.
Results may differ from a plain program's by a relative error of at most 0.000053.
Values sent between devices are 32-bit elements; how exact they have to be, the bound alone decides.
No kernel may reach another device: no remote copies, remote signals or barrier semaphores. Data moves between devices by JAX's collectives and lax.ppermute only.
A program may use at most 128 MiB of HBM per device.

v0:
```python
import jax
import jax.numpy as jnp
from jax import lax
from jax.sharding import PartitionSpec as P

BLK = 256
FRONT = 12288
CHILD = 8192
PANEL = 1024


def from_root(value, axis, source):
    kept = jnp.where(lax.axis_index(axis) == source, value, 0).astype(value.dtype)
    return lax.psum(kept, axis)


def times_transposed(left, right):
    return lax.dot_general(
        left,
        right,
        (((1,), (1,)), ((), ())),
        precision=lax.Precision.HIGHEST,
        preferred_element_type=jnp.float32,
    )


def shards(front_in, child_updates, pattern, child_map, pivot_inverse):
    sub_count = lax.axis_size("sub")
    row_count = lax.axis_size("row")
    col_count = lax.axis_size("col")
    groups = sub_count * col_count
    sub_id = lax.axis_index("sub")
    row_id = lax.axis_index("row")
    col_id = lax.axis_index("col")
    group_id = sub_id * col_count + col_id
    fblocks = FRONT // BLK
    cblocks = CHILD // BLK
    row_blocks = fblocks // row_count
    col_blocks = fblocks // groups
    child_rows = cblocks // row_count
    child_group = cblocks // groups
    child_cols = cblocks // col_count
    updates = child_updates[0].reshape(child_rows, BLK, child_cols, BLK)
    weights = pattern[0].astype(jnp.float32)
    masked = (updates * weights[:, None, :, None]).reshape(
        child_rows * BLK, sub_count, child_group * BLK
    )
    arrived = lax.all_to_all(
        lax.all_to_all(masked, "col", split_axis=1, concat_axis=1, tiled=True),
        "sub",
        split_axis=1,
        concat_axis=1,
        tiled=True,
    )
    rows_map = lax.dynamic_slice_in_dim(child_map, row_id * child_rows, child_rows, 1)
    cols_map = lax.dynamic_slice_in_dim(child_map, group_id * child_group, child_group, 1)
    row_targets = row_id * row_blocks + jnp.arange(row_blocks, dtype=jnp.int32)
    col_targets = group_id * col_blocks + jnp.arange(col_blocks, dtype=jnp.int32)
    row_hot = (rows_map[:, None, :] == row_targets[None, :, None]).astype(jnp.float32)
    col_hot = (cols_map[:, None, :] == col_targets[None, :, None]).astype(jnp.float32)
    pieces = arrived.reshape(child_rows, BLK, sub_count, child_group, BLK)
    spread_rows = jnp.einsum("spa,axsby->pxsby", row_hot, pieces, precision=lax.Precision.HIGHEST)
    extended = jnp.einsum("sqb,pxsby->pxqy", col_hot, spread_rows, precision=lax.Precision.HIGHEST)
    assembled = front_in + extended.reshape(row_blocks * BLK, col_blocks * BLK)
    panel_blocks = PANEL // BLK
    root_count = (panel_blocks + col_blocks - 1) // col_blocks
    gathered = []
    for owner in range(root_count):
        span_blocks = min(col_blocks, panel_blocks - owner * col_blocks)
        received_panel = from_root(assembled[:, : span_blocks * BLK], ("sub", "col"), owner)
        gathered.append(received_panel)
    panel_cols = jnp.concatenate(gathered, axis=1)
    factor = times_transposed(panel_cols, pivot_inverse)
    root_row = group_id * col_blocks // row_blocks
    column_factor = from_root(factor, "row", root_row)
    update = times_transposed(factor, column_factor)
    panel_parts = []
    for column in range(col_blocks):
        global_block = group_id * col_blocks + column
        panel_parts.append(
            lax.dynamic_slice_in_dim(
                factor, jnp.minimum(global_block, panel_blocks - 1) * BLK, BLK, 1
            )
        )
    panel_part = jnp.concatenate(panel_parts, axis=1)
    rows_global = (row_id * row_blocks * BLK + jnp.arange(row_blocks * BLK, dtype=jnp.int32)) // BLK
    cols_global = (
        group_id * col_blocks * BLK + jnp.arange(col_blocks * BLK, dtype=jnp.int32)
    ) // BLK
    below = (rows_global >= panel_blocks)[:, None]
    beyond = (cols_global >= panel_blocks)[None, :]
    result = jnp.where(below & beyond, assembled - update, jnp.where(below, panel_part, assembled))
    return result


def solution(mesh):
    in_specs = (P("row", ("sub", "col")), P("sub", "row", "col"), P("sub", "row", "col"), P(), P())
    out_specs = P("row", ("sub", "col"))
    return jax.shard_map(shards, mesh=mesh, in_specs=in_specs, out_specs=out_specs, check_vma=False)
```

profile of v0, /device:TPU:1, one launch (start us, length us, event | category | flops | bytes accessed | tf_op | source)
XLA Modules:
  0.0 483.1 jit_solution(3434529610521760695)
XLA Ops:
  6.5 0.7 convert_bitcast_fusion
  7.2 2.3 mul.52
  9.5 5.6 %mul.53 = f32[512,4,512]{2,1,0:T(4,128)} reshape(f32[2,256,8,256]{3,2,1,0:T(8,128)} %mul.52) | data formatting | bytes 8388608 | tf_op jit(solution)/shard_map/mul | solution.py:45
  15.2 5.3 %copy.11 = f32[512,4,512]{0,2,1:T(8,128)} copy(f32[512,4,512]{2,1,0:T(4,128)} %mul.53) | data formatting | bytes 8388608 | tf_op jit(solution)/shard_map/mul | solution.py:45
  20.4 5.4 %copy.10 = f32[1,512,2048]{1,2,0:T(8,128)} copy(f32[1,512,2048]{2,1,0:T(8,128)} %param.6) | data formatting | bytes 8388608 | tf_op args[1]
  25.8 6.4 %mul.54 = f32[512,4,512]{0,2,1:T(8,128)} multiply(f32[512,4,512]{0,2,1:T(8,128)} %bitcast.29, f32[512,4,512]{0,2,1:T(8,128)} %copy.11) | non-fusion elementwise | flops 1048576 | bytes 12582912 | tf_op jit(solution)/shard_map/mul | solution.py:45
  32.2 5.2 %copy.12 = f32[512,4,512]{2,0,1:T(8,128)} copy(f32[512,4,512]{0,2,1:T(8,128)} %mul.54) | data formatting | bytes 8388608 | tf_op jit(solution)/shard_map/mul | solution.py:45
  37.5 56.0 %all_to_all.10 = f32[512,4,512]{2,0,1:T(8,128)} all-to-all(f32[512,4,512]{2,0,1:T(8,128)} %copy.12), channel_id=1, replica_groups=mesh['sub'=4,'row'=16,'col'=4] {'col'}, dimensions={1} | all-to-all | bytes 8388608 | tf_op jit(solution)/shard_map/all_to_all | solution.py:49
  93.5 0.0 copy-start.2
  93.5 6.6 %all-to-all-start.1 = ((f32[512,4,512]{2,0,1:T(8,128)}), f32[512,4,512]{2,0,1:T(8,128)}, u32[]{:S(2)}, u32[]{:S(2)}) async-start(f32[512,4,512]{2,0,1:T(8,128)} %all_to_all.10), calls=%async_computation.1 | async-start | bytes 8388608 | tf_op jit(solution)/shard_map/all_to_all | solution.py:48
  100.1 0.0 all-reduce.6.cloned.1.call-start
  100.1 0.0 copy-done.2
  100.1 0.1 constant_dynamic-slice_fusion.3
  100.2 0.1 copy.14
  100.3 93.3 %all-to-all-done.1 = f32[512,4,512]{2,0,1:T(8,128)} async-done(((f32[512,4,512]{2,0,1:T(8,128)}), f32[512,4,512]{2,0,1:T(8,128)}, u32[]{:S(2)}, u32[]{:S(2)}) %all-to-all-start.1) | async-done | bytes 4194336 | tf_op jit(solution)/shard_map/all_to_all | solution.py:48
  193.6 5.9 %reshape.65 = f32[2,256,4,2,256]{4,3,1,0,2:T(2,128)} reshape(f32[512,4,512]{2,0,1:T(8,128)} %all-to-all-done.1) | data formatting | bytes 8388608 | tf_op jit(solution)/shard_map/reshape | solution.py:61
  199.5 13.8 %convolution_bitcast_fusion = f32[3,256,4,2,256]{4,0,3,1,2:T(4,128)S(1)} fusion(f32[2,256,4,2,256]{4,3,1,0,2:T(2,128)} %reshape.65, s32[3]{0:T(128)S(1)} %iota_add_fusion.3, s32[4,2]{1,0:T(4,128)S(1)} %get-tuple-element.13), kind=kOutput, calls=%fused_computation.2 | convolution fusion | flops 37748760 | bytes 10485804 | tf_op jit(solution)/shard_map/spa,axsby->pxsby/dot_general | solution.py:62
  213.3 7.4 %fusion = f32[3,256,256,3,1]{2,3,4,1,0:T(4,128)S(1)} fusion(f32[3,256,4,2,256]{4,0,3,1,2:T(4,128)S(1)} %convolution_bitcast_fusion, s32[4,2]{0,1:T(2,128)S(1)} %copy.14, s32[3]{0:T(128)S(1)} %iota_add_fusion.2), kind=kOutput, calls=%fused_computation | convolution fusion | flops 56623128 | bytes 8650796 | tf_op jit(solution)/shard_map/sqb,pxsby->pxqy/dot_general | solution.py:63
  220.7 0.0 copy-start.1
  220.7 0.6 copy.19
  221.3 1.1 copy-done.1
  222.4 1.7 broadcast_select_fusion.1
  224.1 0.0 copy-start
  224.1 1.5 copy-done
  225.6 0.9 slice_select_fusion
  226.5 0.0 all-reduce.6.cloned.1.call-update
  226.5 0.3 all-reduce.4.cloned.1.call-start
  226.8 117.0 %all-reduce.6.cloned.1.call-done = (f32[768,256]{1,0:T(8,128)}, f32[768,768]{1,0:T(8,128)}) async-done(((f32[768,256]{1,0:T(8,128)}, f32[768,768]{1,0:T(8,128)}), (f32[768,256]{1,0:T(8,128)}, f32[768,768]{1,0:T(8,128)})) %all-reduce.6.cloned.1.call-update) | async-done | bytes 3145744 | tf_op jit(solution)/shard_map/psum | solution.py:14
  343.9 14.4 %broadcast_select_fusion = (f32[768,1024]{1,0:T(8,128)}, f32[768,1024]{1,0:T(8,128)S(1)}) fusion(pred[]{:T(512)S(6)} %eq.43, f32[1024,1024]{1,0:T(8,128)} %param.9, f32[768,256]{1,0:T(8,128)} %get-tuple-element.5, f32[768,768]{1,0:T(8,128)} %get-tuple-element.6), kind=kOutput, calls=%fused_computation.10 | convolution fusion | flops 9665249280 | bytes 13631489 | tf_op jit(solution)/shard_map/dot_general | solution.py:18
  358.3 0.0 all-reduce.4.cloned.1.call-update
  358.3 1.6 constant_dynamic-slice_fusion.2
  359.9 104.4 %all-reduce.4.cloned.1.call-done = f32[768,1024]{1,0:T(8,128)} async-done(((f32[768,1024]{1,0:T(8,128)}), f32[768,1024]{1,0:T(8,128)}) %all-reduce.4.cloned.1.call-update) | async-done | bytes 3145744 | tf_op jit(solution)/shard_map/psum | solution.py:14
  464.4 11.9 %fusion.7 = f32[768,768]{1,0:T(8,128)} fusion(f32[768,768]{1,0:T(8,128)} %copy-done, f32[768,256]{1,0:T(8,128)} %get-tuple-element.10, f32[768,256]{1,0:T(8,128)} %get-tuple-element.11, f32[768,256]{1,0:T(8,128)} %get-tuple-element.9, f32[768,1024]{1,0:T(8,128)S(1)} %get-tuple-element.15, f32[768,1024]{1,0:T(8,128)} %all-reduce.4.cloned.1.call-done, ...), kind=kOutput, calls=%fused_computation.9 | convolution fusion | flops 7251296256 | bytes 13370880 | tf_op jit(solution)/shard_map/dot_general | solution.py:18
  (3 shorter events, 0.0 us)
Async XLA Ops:
  93.5 6.6 %copy-start.2 = (s32[4,32]{1,0:T(4,128)S(1)}, s32[4,32]{1,0:T(4,128)}, u32[]{:S(2)}) copy-start(s32[4,32]{1,0:T(4,128)} %param.8) | copy-start | bytes 1540
  93.5 100.1 %all-to-all-start.1 = ((f32[512,4,512]{2,0,1:T(8,128)}), f32[512,4,512]{2,0,1:T(8,128)}, u32[]{:S(2)}, u32[]{:S(2)}) async-start(f32[512,4,512]{2,0,1:T(8,128)} %all_to_all.10), calls=%async_computation.1 | async-start | bytes 8388608 | tf_op jit(solution)/shard_map/all_to_all | solution.py:48
  100.1 243.8 %all-reduce.6.cloned.1.call-start = ((), (), s32[]{:S(2)}) async-start(), calls=%async_computation.3 | async-start | bytes 6291456 | tf_op jit(solution)/shard_map/psum | solution.py:14
  220.7 1.7 copy-start.1
  224.1 1.5 copy-start
  226.5 237.8 %all-reduce.4.cloned.1.call-start = ((), (), s32[]{:S(2)}) async-start(), calls=%async_computation.2 | async-start | bytes 6291456 | tf_op jit(solution)/shard_map/psum | solution.py:14
Sparse Core Ops, SparseCore 0:
  226.7 117.1 all-reduce.5
  358.4 105.8 all-reduce.3
where the time goes:
time: 484 us; the launch traced here: 483 us
  waiting for transfers between devices  315 us (65%)
  blocking collectives  56 us (12%)
  matrix products  47.5 us (10%)
  local copies, waits for them, and re-layouts  34.6 us (7%)
  between operations  13.5 us (3%)
  other arithmetic  9.79 us (2%)
  starting transfers between devices  6.84 us (1%)
    psum x2, waiting for transfers between devices, from_root(): return lax.psum(kept, axis)  221 us
    all_to_all x1, waiting for transfers between devices, shards(): lax.all_to_all(lax.all_to_all(masked, 'col', split_axis=1, concat_axis=1,...  93.3 us
    all_to_all x1, blocking collectives, shards(): lax.all_to_all(masked, 'col', split_axis=1, concat_axis=1, tiled=True)  56 us
    dot_general x2, matrix products, times_transposed(): lax.dot_general(left, right, (((1,), (1,)), ((), ())), precision=lax.Prec...  26.3 us
    mul x4, local copies, waits for them, and re-layouts, shards(): updates * weights[:, None, :, None]  18.5 us
    dot_general x1, matrix products, shards(): jnp.einsum('spa,axsby->pxsby', row_hot, pieces, precision=lax.Precision.H...  13.8 us
  transfers between devices with their start and end apart: 3, of which 3 were waited for; matrix products, arithmetic and copies ran while one was open for 0% of the time, Pallas kernels for 0%

commit v1 on v0

--- a/solution.py
+++ b/solution.py
@@ -9,9 +9,13 @@
 PANEL = 1024
 
 
+def play_marks_in(original, axis_name):
+    return jnp.sum(lax.all_gather(original, axis_name=axis_name), axis=0)
+
+
 def from_root(value, axis, source):
     kept = jnp.where(lax.axis_index(axis) == source, value, 0).astype(value.dtype)
-    return lax.psum(kept, axis)
+    return play_marks_in(kept, axis)
 
 
 def times_transposed(left, right):

time: 484 us -> 851 us (1.76)
  waiting for transfers between devices: 315 us -> 641 us
  other arithmetic: 9.79 us -> 50.5 us
    all_gather x0 -> x3, waiting for transfers between devices: none -> 547 us  [play_marks_in(): return jnp.sum(lax.all_gather(original, axis_name=axis_name), axis=0)]
    psum x2 -> x0, waiting for transfers between devices: 221 us -> none  [from_root(): return lax.psum(kept, axis)]
    reduce_sum x0 -> x3, other arithmetic: none -> 40.7 us  [play_marks_in(): return jnp.sum(lax.all_gather(original, axis_name=axis_name), axis=0)]
  transfers between devices with their start and end apart: 3 -> 4, of which waited for: 3 -> 4; matrix products, arithmetic and copies ran while one was open for 0% -> 1% of each run, Pallas kernels for 0% -> 0%
where the time goes in v1:
time: 851 us; the launch traced here: 850 us
  waiting for transfers between devices  641 us (75%)
  blocking collectives  56 us (7%)
  other arithmetic  50.5 us (6%)
  matrix products  47.5 us (6%)
  local copies, waits for them, and re-layouts  34.4 us (4%)
  between operations  13.2 us (2%)
    all_gather x3, waiting for transfers between devices, play_marks_in(): return jnp.sum(lax.all_gather(original, axis_name=axis_name), axis=0)  547 us
    all_to_all x1, waiting for transfers between devices, shards(): lax.all_to_all(lax.all_to_all(masked, 'col', split_axis=1, concat_axis=1,...  93.3 us
    all_to_all x1, blocking collectives, shards(): lax.all_to_all(masked, 'col', split_axis=1, concat_axis=1, tiled=True)  56 us
    reduce_sum x3, other arithmetic, play_marks_in(): return jnp.sum(lax.all_gather(original, axis_name=axis_name), axis=0)  40.7 us
    dot_general x2, matrix products, times_transposed(): lax.dot_general(left, right, (((1,), (1,)), ((), ())), precision=lax.Prec...  26.3 us
    mul x4, local copies, waits for them, and re-layouts, shards(): updates * weights[:, None, :, None]  18.4 us
  transfers between devices with their start and end apart: 4, of which 4 were waited for; matrix products, arithmetic and copies ran while one was open for 1% of the time, Pallas kernels for 0%

profile of v1, /device:TPU:1, one launch (start us, length us, event | category | flops | bytes accessed | tf_op | source)
XLA Modules:
  0.0 850.0 jit_solution(13432269740062558481)
XLA Ops:
  6.5 0.7 convert_bitcast_fusion
  7.2 2.3 mul.52
  9.5 5.6 mul.53
  15.2 5.3 copy.11
  20.4 5.4 copy.10
  25.8 6.5 mul.54
  32.2 5.2 copy.12
  37.5 56.0 %all_to_all.10 = f32[512,4,512]{2,0,1:T(8,128)} all-to-all(f32[512,4,512]{2,0,1:T(8,128)} %copy.12), channel_id=1, replica_groups=mesh['sub'=4,'row'=16,'col'=4] {'col'}, dimensions={1} | all-to-all | bytes 8388608 | tf_op jit(solution)/shard_map/all_to_all | solution.py:53
  93.5 0.0 copy-start.2
  93.5 6.6 all-to-all-start.1
  100.1 0.0 all-gather.9.cloned.1.call-start
  100.1 0.0 copy-done.2
  100.1 0.1 constant_dynamic-slice_fusion.3
  100.2 0.1 copy.14
  100.3 93.3 %all-to-all-done.1 = f32[512,4,512]{2,0,1:T(8,128)} async-done(((f32[512,4,512]{2,0,1:T(8,128)}), f32[512,4,512]{2,0,1:T(8,128)}, u32[]{:S(2)}, u32[]{:S(2)}) %all-to-all-start.1) | async-done | bytes 4194336 | tf_op jit(solution)/shard_map/all_to_all | solution.py:52
  193.6 5.9 reshape.65
  199.5 13.8 %convolution_bitcast_fusion = f32[3,256,4,2,256]{4,0,3,1,2:T(4,128)S(1)} fusion(f32[2,256,4,2,256]{4,3,1,0,2:T(2,128)} %reshape.65, s32[3]{0:T(128)S(1)} %iota_add_fusion.3, s32[4,2]{1,0:T(4,128)S(1)} %get-tuple-element.11), kind=kOutput, calls=%fused_computation.2 | convolution fusion | flops 37748760 | bytes 10485804 | tf_op jit(solution)/shard_map/spa,axsby->pxsby/dot_general | solution.py:66
  213.3 7.4 fusion
  220.7 0.0 copy-start.1
  220.7 0.6 copy.19
  221.3 1.1 copy-done.1
  222.4 1.7 broadcast_select_fusion.1
  224.1 0.0 copy-start
  224.1 1.4 copy-done
  225.5 0.9 slice_select_fusion
  226.4 0.0 all-gather.9.cloned.1.call-update
  226.4 0.0 all-gather.7.cloned.1.call-start
  226.5 0.7 all-gather.7.cloned.1.call-update
  227.2 0.3 all-gather.11.cloned.1.call-start
  227.5 74.6 %all-gather.9.cloned.1.call-done = f32[12288,256]{1,0:T(8,128)} async-done(((f32[768,256]{1,0:T(8,128)}), f32[12288,256]{1,0:T(8,128)}) %all-gather.9.cloned.1.call-update) | async-done | bytes 12582928 | tf_op jit(solution)/shard_map/all_gather | solution.py:13
  302.1 6.3 reduce_sum.28
  308.4 188.2 %all-gather.7.cloned.1.call-done = f32[12288,768]{1,0:T(8,128)} async-done(((f32[768,768]{1,0:T(8,128)}), f32[12288,768]{1,0:T(8,128)}) %all-gather.7.cloned.1.call-update) | async-done | bytes 37748752 | tf_op jit(solution)/shard_map/all_gather | solution.py:13
  496.6 15.1 %reduce_sum.27 = f32[768,768]{1,0:T(8,128)} reduce(f32[16,768,768]{2,1,0:T(8,128)} %bitcast.33, f32[]{:T(128)} %constant.59.clone.1), dimensions={0}, to_apply=%region_0.1 | reduce | flops 8847360 | bytes 40108036 | tf_op jit(solution)/shard_map/reduce_sum | solution.py:13
  511.8 14.4 %broadcast_select_fusion = (f32[768,1024]{1,0:T(8,128)}, f32[768,1024]{1,0:T(8,128)S(1)}) fusion(pred[]{:T(512)S(6)} %eq.43, f32[1024,1024]{1,0:T(8,128)} %param.9, f32[768,256]{1,0:T(8,128)} %reduce_sum.28, f32[768,768]{1,0:T(8,128)} %reduce_sum.27), kind=kOutput, calls=%fused_computation.10 | convolution fusion | flops 9665249280 | bytes 13631489 | tf_op jit(solution)/shard_map/dot_general | solution.py:22
  526.1 0.0 all-gather.11.cloned.1.call-update
  526.2 1.5 constant_dynamic-slice_fusion.2
  527.7 284.6 %all-gather.11.cloned.1.call-done = f32[12288,1024]{1,0:T(8,128)} async-done(((f32[768,1024]{1,0:T(8,128)}), f32[12288,1024]{1,0:T(8,128)}) %all-gather.11.cloned.1.call-update) | async-done | bytes 50331664 | tf_op jit(solution)/shard_map/all_gather | solution.py:13
  812.3 19.2 %reduce_sum.29 = f32[768,1024]{1,0:T(8,128)} reduce(f32[16,768,1024]{2,1,0:T(8,128)} %bitcast.32, f32[]{:T(128)} %constant.59.clone.1), dimensions={0}, to_apply=%region_2.3 | reduce | flops 11796480 | bytes 53477380 | tf_op jit(solution)/shard_map/reduce_sum | solution.py:13
  831.6 11.9 %fusion.7 = f32[768,768]{1,0:T(8,128)} fusion(f32[768,768]{1,0:T(8,128)} %copy-done, f32[768,256]{1,0:T(8,128)} %get-tuple-element.8, f32[768,256]{1,0:T(8,128)} %get-tuple-element.9, f32[768,256]{1,0:T(8,128)} %get-tuple-element.7, f32[768,1024]{1,0:T(8,128)S(1)} %get-tuple-element.13, f32[768,1024]{1,0:T(8,128)} %reduce_sum.29, ...), kind=kOutput, calls=%fused_computation.9 | convolution fusion | flops 7251296256 | bytes 13370880 | tf_op jit(solution)/shard_map/dot_general | solution.py:22
  (4 shorter events, 0.0 us)
Async XLA Ops:
  93.5 6.6 copy-start.2
  93.5 100.1 %all-to-all-start.1 = ((f32[512,4,512]{2,0,1:T(8,128)}), f32[512,4,512]{2,0,1:T(8,128)}, u32[]{:S(2)}, u32[]{:S(2)}) async-start(f32[512,4,512]{2,0,1:T(8,128)} %all_to_all.10), calls=%async_computation.1 | async-start | bytes 8388608 | tf_op jit(solution)/shard_map/all_to_all | solution.py:52
  100.1 202.0 %all-gather.9.cloned.1.call-start = ((), (), s32[]{:S(2)}) async-start(), calls=%async_computation.3 | async-start | bytes 13369344 | tf_op jit(solution)/shard_map/all_gather | solution.py:13
  220.7 1.7 copy-start.1
  224.1 1.4 copy-start
  226.4 270.2 %all-gather.7.cloned.1.call-start = ((), (), s32[]{:S(2)}) async-start(), calls=%async_computation.2 | async-start | bytes 40108032 | tf_op jit(solution)/shard_map/all_gather | solution.py:13
  227.2 585.1 %all-gather.11.cloned.1.call-start = ((), (), s32[]{:S(2)}) async-start(), calls=%async_computation.4 | async-start | bytes 53477376 | tf_op jit(solution)/shard_map/all_gather | solution.py:13
Sparse Core Ops, SparseCore 0:
  226.6 75.4 all-gather.8
  303.9 192.6 all-gather.6
  526.3 286.0 all-gather.10
